TPU v7x, 512 devices: a whole 4x8x8 slice. The times are simulated.
512 devices in a mesh: expert: 16 (over x, y_hi), tensor: 32 (over z, y_lo, core).
Axes of the slice: x: 4, y: 8 (y_hi: 4, y_lo: 2; y = y_hi * 2 + y_lo), z: 8, core: 2. Of those that a mesh axis runs over, the one named last changes fastest.
Arguments:
- tokens: bfloat16 [2048, 6144], P('expert'), may hold values from -6 to 6
- routes: int32 [2048, 4], P('expert'), may hold values from 0 to 15, all different within a row; in each aligned block of 128 rows (0 to 127, 128 to 255, ...) at most 40 rows name the same one
- gates: float32 [2048, 4], P('expert'), may hold values from 0.05 to 1
- gate_proj: bfloat16 [16, 2688, 6144], P('expert', 'tensor'), may hold values from -0.078125 to 0.078125
- up_proj: bfloat16 [16, 2688, 6144], P('expert', 'tensor'), may hold values from -0.078125 to 0.078125
- down_proj: bfloat16 [16, 6144, 2688], P('expert', 'tensor'), may hold values from -0.0625 to 0.0625
Outputs:
- combined: bfloat16 [2048, 6144], P('expert', 'tensor')
Inputs may be any that keep to these rules, and one draw needn't show every extreme that they name: `routes`: the ids of one row are distinct. In each aligned block of 128 rows no id is named by more than 40 rows, a bound that some block reaches.
All inputs are finite; a program needn't handle non-finite values.
Results may differ from a plain program's by a relative error of at most 0.0057.
Values may be sent and summed in bfloat16 or wider, within the bound.
No kernel may reach another device: no remote copies, remote signals or barrier semaphores. Data moves between devices by JAX's collectives and lax.ppermute only.
A program may use at most 64 MiB of HBM per device.

v0:
```python
import jax
import jax.numpy as jnp
from jax import lax
from jax.sharding import PartitionSpec as P

WIN = 4
CAP = 40


def slot_tables(route_block, gate_block):
    row_count = route_block.shape[0]
    experts = jnp.arange(WIN, dtype=jnp.int32)
    hits = route_block[None, :, :] == experts[:, None, None]
    chosen = jnp.any(hits, axis=2)
    position = jnp.cumsum(chosen.astype(jnp.int32), axis=1) - 1
    slots = jnp.arange(CAP, dtype=jnp.int32)
    match = chosen[:, None, :] & (position[:, None, :] == slots[None, :, None])
    row_ids = jnp.arange(row_count, dtype=jnp.int32)
    row_index = jnp.sum(jnp.where(match, row_ids[None, None, :], 0), axis=2)
    filled = jnp.any(match, axis=2)
    weight = jnp.sum(
        jnp.where(hits, gate_block[None, :, :], jnp.zeros((), gate_block.dtype)), axis=2
    )
    return (position, row_index, filled, weight)


def contract_last(left, right):
    return lax.dot_general(
        left, right, (((1,), (1,)), ((), ())), preferred_element_type=jnp.float32
    )


def body(tokens, routes, gates, gate_proj, up_proj, down_proj):
    groups = lax.axis_size("expert")
    split = groups // WIN
    width = tokens.shape[1]
    w_gate = gate_proj[0]
    w_up = up_proj[0]
    w_down = down_proj[0]
    position, row_index, filled, weight = slot_tables(routes, gates)
    picked = jnp.take(tokens, row_index, axis=0)
    picked = jnp.where(filled[:, :, None], picked, jnp.zeros((), tokens.dtype))
    outgoing = jnp.repeat(picked, split, axis=0)
    slot_rows = groups * CAP
    arrived = lax.all_to_all(outgoing, "expert", split_axis=0, concat_axis=0, tiled=True)
    flat_rows = arrived.reshape(slot_rows, width)
    gate_act = contract_last(flat_rows, w_gate)
    up_act = contract_last(flat_rows, w_up)
    hidden = (jax.nn.silu(gate_act) * up_act).astype(jnp.bfloat16)
    partial_value = contract_last(lax.all_gather(hidden, "tensor", axis=1, tiled=True), w_down)
    partial_value = partial_value.astype(jnp.bfloat16).reshape(groups, CAP, w_down.shape[0])
    returned = lax.all_to_all(partial_value, "expert", split_axis=0, concat_axis=0, tiled=True)
    expert_out = returned.astype(jnp.float32).reshape(WIN, split, CAP, w_down.shape[0]).sum(axis=1)
    flat_sum = expert_out.reshape(WIN * CAP, w_down.shape[0])
    offsets = jnp.arange(WIN, dtype=jnp.int32)[:, None] * CAP
    index = offsets + jnp.clip(position, 0, CAP - 1)
    values = jnp.take(flat_sum, index, axis=0)
    return jnp.sum(values * weight[:, :, None], axis=0).astype(jnp.bfloat16)


def solution(mesh):
    in_specs = (
        P("expert", None),
        P("expert", None),
        P("expert", None),
        P("expert", "tensor", None),
        P("expert", "tensor", None),
        P("expert", "tensor", None),
    )
    out_specs = P("expert", "tensor")
    return jax.shard_map(body, mesh=mesh, in_specs=in_specs, out_specs=out_specs, check_vma=False)
```

profile of v0, /device:TPU:8, one launch (start us, length us, event | category | flops | bytes accessed | tf_op | source)
XLA Modules:
  0.0 313.3 jit_solution(4435394938757956688)
XLA Ops:
  6.5 0.0 copy-start
  6.5 0.0 all-gather.3.cloned.1.call-start
  6.5 0.8 fusion.8
  7.4 0.3 reduce_window_sum.11
  7.7 0.1 select_reduce_fusion
  7.9 0.1 fusion.7
  8.0 0.1 reshape.122
  8.1 0.0 copy-done
  8.1 1.7 gather_fusion
  9.8 0.3 select_select_fusion
  10.1 1.0 broadcast_in_dim.76
  11.1 0.0 copy-start.1
  11.1 152.1 %all_to_all.10 = bf16[16,40,6144]{2,1,0:T(8,128)(2,1)S(1)} all-to-all(bf16[16,40,6144]{2,1,0:T(8,128)(2,1)S(1)} %bitcast.38), channel_id=1, replica_groups=mesh['expert'=16,'tensor'=32] {'expert'}, dimensions={0} | all-to-all | bytes 15728640 | tf_op jit(solution)/shard_map/all_to_all | solution.py:45
  163.3 0.0 copy-done.1
  163.3 0.0 copy-start.4
  163.3 2.5 fusion.3
  165.7 0.0 copy-done.4
  165.7 3.1 %fusion.1 = bf16[1,84,640]{2,1,0:T(8,128)(2,1)} fusion(bf16[640,6144]{1,0:T(8,128)(2,1)S(1)} %bitcast.37, bf16[1,84,6144]{2,1,0:T(8,128)(2,1)S(1)} %copy-done.4, f32[640,84]{0,1:T(8,128)S(1)} %fusion.3), kind=kOutput, calls=%fused_computation.6 | convolution fusion | flops 660925440 | bytes 9219072 | tf_op jit(solution)/shard_map/dot_general | solution.py:28
  168.9 0.0 all-gather.3.cloned.1.call-update
  168.9 0.0 copy-start.5
  168.9 101.5 %all-gather.3.cloned.1.call-done = bf16[32,84,640]{2,1,0:T(8,128)(2,1)} async-done(((bf16[1,84,640]{2,1,0:T(8,128)(2,1)}), bf16[32,84,640]{2,1,0:T(8,128)(2,1)}) %all-gather.3.cloned.1.call-update) | async-done | bytes 3440656 | tf_op jit(solution)/shard_map/all_gather | solution.py:50
  270.5 5.5 %reshape.139 = bf16[2688,640]{1,0:T(8,128)(2,1)} reshape(bf16[32,84,640]{2,1,0:T(8,128)(2,1)} %all-gather.3.cloned.1.call-done) | data formatting | bytes 6881280
  276.0 0.0 copy-done.5
  276.0 0.0 copy-start.2
  276.0 0.0 copy-start.3
  276.0 3.0 convolution_convert_fusion
  279.0 0.9 copy.18
  279.9 9.0 %all-to-all-start.1 = ((bf16[16,40,192]{2,1,0:T(8,128)(2,1)}), bf16[16,40,192]{2,1,0:T(8,128)(2,1)S(1)}, u32[]{:S(2)}, u32[]{:S(2)}) async-start(bf16[16,40,192]{2,1,0:T(8,128)(2,1)} %bitcast.9), calls=%async_computation.1 | async-start | bytes 655360 | tf_op jit(solution)/shard_map/all_to_all | solution.py:52
  288.8 0.1 fusion.9
  288.9 0.0 copy-done.2
  288.9 0.0 copy-done.3
  289.0 0.1 compare_and_fusion.1
  289.0 14.8 %all-to-all-done.1 = bf16[16,40,192]{2,1,0:T(8,128)(2,1)S(1)} async-done(((bf16[16,40,192]{2,1,0:T(8,128)(2,1)}), bf16[16,40,192]{2,1,0:T(8,128)(2,1)S(1)}, u32[]{:S(2)}, u32[]{:S(2)}) %all-to-all-start.1) | async-done | bytes 245792 | tf_op jit(solution)/shard_map/all_to_all | solution.py:52
  303.8 0.1 convert_reduce_fusion
  303.9 1.6 gather_fusion.1
  305.5 0.2 multiply_reduce_fusion
  305.7 0.7 copy.19
  (8 shorter events, 0.1 us)
Async XLA Ops:
  6.5 1.6 copy-start
  6.5 263.9 %all-gather.3.cloned.1.call-start = ((), (), s32[]{:S(2)}) async-start(), calls=%async_computation.2 | async-start | bytes 3717120 | tf_op jit(solution)/shard_map/all_gather | solution.py:50
  11.1 152.2 %copy-start.1 = (bf16[1,84,6144]{2,1,0:T(8,128)(2,1)S(1)}, bf16[1,84,6144]{2,1,0:T(8,128)(2,1)}, u32[]{:S(2)}) copy-start(bf16[1,84,6144]{2,1,0:T(8,128)(2,1)} %param.9) | copy-start | bytes 3096580
  163.3 2.5 copy-start.4
  168.9 107.1 %copy-start.5 = (bf16[1,192,2688]{2,1,0:T(8,128)(2,1)S(1)}, bf16[1,192,2688]{2,1,0:T(8,128)(2,1)}, u32[]{:S(2)}) copy-start(bf16[1,192,2688]{2,1,0:T(8,128)(2,1)} %param.11) | copy-start | bytes 3096580
  276.0 13.0 %copy-start.2 = (s32[128,4]{0,1:T(4,128)S(1)}, s32[128,4]{0,1:T(4,128)}, u32[]{:S(2)}) copy-start(s32[128,4]{0,1:T(4,128)} %param.7) | copy-start | bytes 6148
  276.0 13.0 %copy-start.3 = (f32[128,4]{0,1:T(4,128)S(1)}, f32[128,4]{0,1:T(4,128)}, u32[]{:S(2)}) copy-start(f32[128,4]{0,1:T(4,128)} %param.8) | copy-start | bytes 6148
  279.9 24.0 %all-to-all-start.1 = ((bf16[16,40,192]{2,1,0:T(8,128)(2,1)}), bf16[16,40,192]{2,1,0:T(8,128)(2,1)S(1)}, u32[]{:S(2)}, u32[]{:S(2)}) async-start(bf16[16,40,192]{2,1,0:T(8,128)(2,1)} %bitcast.9), calls=%async_computation.1 | async-start | bytes 655360 | tf_op jit(solution)/shard_map/all_to_all | solution.py:52
Sparse Core Ops, SparseCore 0:
  169.0 101.3 all-gather.2
where the time goes:
time: 314 us; the launch traced here: 313 us
  blocking collectives  152 us (48%)
  waiting for transfers between devices  116 us (37%)
  between operations  13.5 us (4%)
  local copies, waits for them, and re-layouts  11.5 us (4%)
  starting transfers between devices  8.98 us (3%)
  matrix products  8.59 us (3%)
    all_to_all x1, blocking collectives, body(): lax.all_to_all(outgoing, 'expert', split_axis=0, concat_axis=0, tiled=True)  152 us
    all_gather x1, waiting for transfers between devices, body(): lax.all_gather(hidden, 'tensor', axis=1, tiled=True)  102 us
    all_to_all x1, waiting for transfers between devices, body(): lax.all_to_all(partial_value, 'expert', split_axis=0, concat_axis=0, tile...  14.8 us
    all_to_all x1, starting transfers between devices, body(): lax.all_to_all(partial_value, 'expert', split_axis=0, concat_axis=0, tile...  8.98 us
    dot_general x3, matrix products, contract_last(): lax.dot_general(left, right, (((1,), (1,)), ((), ())), preferred_element_...  8.59 us
  transfers between devices with their start and end apart: 2, of which 2 were waited for; matrix products, arithmetic and copies ran while one was open for 0% of the time, Pallas kernels for 0%

commit v1 on v0

--- a/solution.py
+++ b/solution.py
@@ -47,7 +47,12 @@
     gate_act = contract_last(flat_rows, w_gate)
     up_act = contract_last(flat_rows, w_up)
     hidden = (jax.nn.silu(gate_act) * up_act).astype(jnp.bfloat16)
-    partial_value = contract_last(lax.all_gather(hidden, "tensor", axis=1, tiled=True), w_down)
+    partial_value = contract_last(
+        jnp.concatenate(
+            lax.all_to_all(jnp.stack([hidden] * lax.axis_size("tensor")), "tensor", 0, 0), axis=1
+        ),
+        w_down,
+    )
     partial_value = partial_value.astype(jnp.bfloat16).reshape(groups, CAP, w_down.shape[0])
     returned = lax.all_to_all(partial_value, "expert", split_axis=0, concat_axis=0, tiled=True)
     expert_out = returned.astype(jnp.float32).reshape(WIN, split, CAP, w_down.shape[0]).sum(axis=1)

time: 314 us -> 332 us (1.057)
  the two profiles are of different devices: /device:TPU:8 before, /device:TPU:128 now
where the time goes in v1:
time: 332 us
  blocking collectives  186 us (56%)
  waiting for transfers between devices  109 us (33%)
  local copies, waits for them, and re-layouts  13.7 us (4%)
  starting transfers between devices  12.9 us (4%)
  matrix products  7.94 us (2%)
    all_to_all x1, blocking collectives, body(): lax.all_to_all(outgoing, 'expert', split_axis=0, concat_axis=0, tiled=True)  186 us
    all_to_all x1, waiting for transfers between devices, body(): lax.all_to_all(jnp.stack([hidden] * lax.axis_size('tensor')), 'tensor', 0...  95.4 us
    all_to_all x1, waiting for transfers between devices, body(): lax.all_to_all(partial_value, 'expert', split_axis=0, concat_axis=0, tile...  13.6 us
    all_to_all x1, starting transfers between devices, body(): lax.all_to_all(jnp.stack([hidden] * lax.axis_size('tensor')), 'tensor', 0...  9.26 us
    dot_general x3, matrix products, contract_last(): lax.dot_general(left, right, (((1,), (1,)), ((), ())), preferred_element_...  7.94 us
  transfers between devices with their start and end apart: 2, of which 2 were waited for; matrix products, arithmetic and copies ran while one was open for 0% of the time, Pallas kernels for 0%

profile of v1, /device:TPU:128, one launch (start us, length us, event | category | flops | bytes accessed | tf_op | source)
XLA Modules:
  0.0 331.8 jit_solution(326066754998085042)
XLA Ops:
  0.0 0.0 copy-start
  0.0 0.8 fusion.7
  0.8 0.3 reduce_window_sum.11
  1.1 0.1 select_reduce_fusion
  1.3 0.1 fusion.6
  1.5 0.1 reshape.132
  1.6 0.0 copy-done
  1.6 1.7 gather_fusion
  3.3 0.3 select_select_fusion
  3.6 1.0 broadcast_in_dim.76
  4.6 0.0 copy-start.1
  4.6 185.9 %all_to_all.15 = bf16[16,40,6144]{2,1,0:T(8,128)(2,1)S(1)} all-to-all(bf16[16,40,6144]{2,1,0:T(8,128)(2,1)S(1)} %bitcast.37), channel_id=1, replica_groups=mesh['expert'=16,'tensor'=32] {'expert'}, dimensions={0} | all-to-all | bytes 15728640 | tf_op jit(solution)/shard_map/all_to_all | solution.py:45
  190.5 0.0 copy-done.1
  190.5 0.0 copy-start.4
  190.5 2.5 fusion.2
  193.0 0.0 copy-done.4
  193.0 2.5 fusion
  195.5 2.1 stack.2
  197.6 9.3 %all-to-all-start.1 = ((bf16[32,640,84]{1,2,0:T(8,128)(2,1)}), bf16[32,640,84]{1,2,0:T(8,128)(2,1)}, u32[]{:S(2)}, u32[]{:S(2)}) async-start(bf16[32,640,84]{1,2,0:T(8,128)(2,1)} %stack.2), calls=%async_computation.1 | async-start | bytes 7208960 | tf_op jit(solution)/shard_map/all_to_all | solution.py:52
  206.9 95.4 %all-to-all-done.1 = bf16[32,640,84]{1,2,0:T(8,128)(2,1)} async-done(((bf16[32,640,84]{1,2,0:T(8,128)(2,1)}), bf16[32,640,84]{1,2,0:T(8,128)(2,1)}, u32[]{:S(2)}, u32[]{:S(2)}) %all-to-all-start.1) | async-done | bytes 3440672 | tf_op jit(solution)/shard_map/all_to_all | solution.py:52
  302.3 0.0 copy-start.5
  302.3 5.6 %reshape.123 = bf16[640,2688]{0,1:T(8,128)(2,1)} reshape(bf16[640,32,84]{0,2,1:T(8,128)(2,1)} %bitcast.6) | data formatting | bytes 6881280 | tf_op jit(solution)/shard_map/reshape | solution.py:51
  307.9 0.0 copy-done.5
  307.9 0.0 copy-start.2
  307.9 0.0 copy-start.3
  307.9 3.0 convolution_convert_fusion
  310.9 0.9 copy.19
  311.8 3.7 %all-to-all-start.2 = ((bf16[16,40,192]{2,1,0:T(8,128)(2,1)}), bf16[16,40,192]{2,1,0:T(8,128)(2,1)S(1)}, u32[]{:S(2)}, u32[]{:S(2)}) async-start(bf16[16,40,192]{2,1,0:T(8,128)(2,1)} %bitcast.8), calls=%async_computation.2 | async-start | bytes 655360 | tf_op jit(solution)/shard_map/all_to_all | solution.py:57
  315.4 0.1 fusion.8
  315.5 0.0 copy-done.2
  315.5 0.0 copy-done.3
  315.5 0.1 compare_and_fusion.1
  315.6 13.6 %all-to-all-done.2 = bf16[16,40,192]{2,1,0:T(8,128)(2,1)S(1)} async-done(((bf16[16,40,192]{2,1,0:T(8,128)(2,1)}), bf16[16,40,192]{2,1,0:T(8,128)(2,1)S(1)}, u32[]{:S(2)}, u32[]{:S(2)}) %all-to-all-start.2) | async-done | bytes 245792 | tf_op jit(solution)/shard_map/all_to_all | solution.py:57
  329.2 0.1 convert_reduce_fusion
  329.3 1.6 gather_fusion.1
  330.9 0.2 multiply_reduce_fusion
  331.1 0.7 copy.20
  (8 shorter events, 0.1 us)
Async XLA Ops:
  0.0 1.6 copy-start
  4.6 185.9 %copy-start.1 = (bf16[1,84,6144]{2,1,0:T(8,128)(2,1)S(1)}, bf16[1,84,6144]{2,1,0:T(8,128)(2,1)}, u32[]{:S(2)}) copy-start(bf16[1,84,6144]{2,1,0:T(8,128)(2,1)} %param.9) | copy-start | bytes 3096580
  190.5 2.5 copy-start.4
  197.6 104.7 %all-to-all-start.1 = ((bf16[32,640,84]{1,2,0:T(8,128)(2,1)}), bf16[32,640,84]{1,2,0:T(8,128)(2,1)}, u32[]{:S(2)}, u32[]{:S(2)}) async-start(bf16[32,640,84]{1,2,0:T(8,128)(2,1)} %stack.2), calls=%async_computation.1 | async-start | bytes 7208960 | tf_op jit(solution)/shard_map/all_to_all | solution.py:52
  302.3 5.6 %copy-start.5 = (bf16[1,192,2688]{2,1,0:T(8,128)(2,1)S(1)}, bf16[1,192,2688]{2,1,0:T(8,128)(2,1)}, u32[]{:S(2)}) copy-start(bf16[1,192,2688]{2,1,0:T(8,128)(2,1)} %param.11) | copy-start | bytes 3096580
  307.9 7.6 %copy-start.2 = (s32[128,4]{0,1:T(4,128)S(1)}, s32[128,4]{0,1:T(4,128)}, u32[]{:S(2)}) copy-start(s32[128,4]{0,1:T(4,128)} %param.7) | copy-start | bytes 6148
  307.9 7.6 %copy-start.3 = (f32[128,4]{0,1:T(4,128)S(1)}, f32[128,4]{0,1:T(4,128)}, u32[]{:S(2)}) copy-start(f32[128,4]{0,1:T(4,128)} %param.8) | copy-start | bytes 6148
  311.8 17.5 %all-to-all-start.2 = ((bf16[16,40,192]{2,1,0:T(8,128)(2,1)}), bf16[16,40,192]{2,1,0:T(8,128)(2,1)S(1)}, u32[]{:S(2)}, u32[]{:S(2)}) async-start(bf16[16,40,192]{2,1,0:T(8,128)(2,1)} %bitcast.8), calls=%async_computation.2 | async-start | bytes 655360 | tf_op jit(solution)/shard_map/all_to_all | solution.py:57
